TPU v7x, 32 devices: a whole 2x2x4 slice. The times are simulated.
32 devices in a mesh: dp: 2 (over y), expert: 4 (over x, core), tensor: 4 (over z).
Axes of the slice: x: 2, y: 2, z: 4, core: 2. Of those that a mesh axis runs over, the one named last changes fastest.
Arguments:
- hidden_states: bfloat16 [256, 4096], P(('dp', 'expert'), 'tensor'), may hold values from -6 to 6
- chosen_experts: int32 [256, 2], P(('dp', 'expert')), may hold values from 0 to 3, all different within a row; in each aligned block of 32 rows (0 to 31, 32 to 63, ...) at most 16 rows name the same one
- choice_weights: float32 [256, 2], P(('dp', 'expert')), may hold values from 0.2 to 1
- gate_proj: bfloat16 [4, 4096, 8192], P('expert', None, ('dp', 'tensor')), may hold values from -0.09375 to 0.09375
- up_proj: bfloat16 [4, 4096, 8192], P('expert', None, ('dp', 'tensor')), may hold values from -0.09375 to 0.09375
- down_proj: bfloat16 [4, 8192, 4096], P('expert', 'dp', 'tensor'), may hold values from -0.0625 to 0.0625
Outputs:
- moe_output: bfloat16 [256, 4096], P(('dp', 'expert'), 'tensor')
Inputs may be any that keep to these rules, and one draw needn't show every extreme that they name: `chosen_experts`: each row names 2 different experts; among the 32 rows of one device no expert is named more than 16 times, a bound that some block reaches.
All inputs are finite; a program needn't handle non-finite values.
Results may differ from a plain program's by a relative error of at most 0.0058.
Values may be sent and summed in bfloat16 or wider, within the bound.
A program may use at most 64 MiB of HBM per device.

v0:
```python
import jax
import jax.numpy as jnp
from jax import lax
from jax.sharding import PartitionSpec as P

CAP = 16


def slot_tables(chosen_experts, experts, capacity):
    flat_ids = chosen_experts.reshape(-1)
    onehot = (flat_ids[:, None] == jnp.arange(experts, dtype=jnp.int32)[None, :]).astype(jnp.int32)
    before = jnp.cumsum(onehot, axis=0) - onehot
    position = jnp.sum(before * onehot, axis=1)
    return (flat_ids * capacity + position).reshape(chosen_experts.shape)


def body(hidden_states, chosen_experts, choice_weights, gate_proj, up_proj, down_proj):
    experts = lax.axis_size("expert")
    token_count = hidden_states.shape[0]
    feat_width = hidden_states.shape[1]
    slot_count = experts * CAP
    target = slot_tables(chosen_experts, experts, CAP)
    slot_ids = jnp.arange(slot_count, dtype=jnp.int32)
    placing = jnp.zeros((slot_count, token_count), jnp.float32)
    weights_table = jnp.zeros((token_count, slot_count), jnp.float32)
    for column in range(target.shape[1]):
        placing = placing + (slot_ids[:, None] == target[None, :, column]).astype(jnp.float32)
        weights_table = weights_table + jnp.where(
            target[:, column][:, None] == slot_ids[None, :],
            choice_weights[:, column][:, None],
            jnp.float32(0.0),
        )
    packed = jnp.dot(
        placing.astype(jnp.bfloat16), hidden_states, preferred_element_type=jnp.float32
    )
    packed = packed.astype(jnp.bfloat16).reshape(experts, CAP, feat_width)
    arrived = lax.all_to_all(packed, "expert", split_axis=0, concat_axis=0, tiled=True).reshape(
        slot_count, feat_width
    )
    gate_weights = gate_proj[0]
    up_weights = up_proj[0]
    down_weights = down_proj[0]
    features = lax.all_gather(arrived, "tensor", axis=1, tiled=True)
    shards = lax.all_gather(features, "dp", axis=0, tiled=True)
    gate_part = jnp.dot(shards, gate_weights, preferred_element_type=jnp.float32)
    up_part = jnp.dot(shards, up_weights, preferred_element_type=jnp.float32)
    activated = (jax.nn.silu(gate_part) * up_part).astype(jnp.bfloat16)
    unit_rows = lax.all_gather(activated, "tensor", axis=1, tiled=True)
    summed = lax.psum_scatter(
        jnp.dot(unit_rows, down_weights, preferred_element_type=jnp.float32),
        "dp",
        scatter_dimension=0,
        tiled=True,
    )
    outgoing = summed.astype(jnp.bfloat16).reshape(experts, CAP, feat_width)
    returned = lax.all_to_all(outgoing, "expert", split_axis=0, concat_axis=0, tiled=True).reshape(
        slot_count, feat_width
    )
    combined = jnp.dot(
        weights_table,
        returned.astype(jnp.float32),
        precision=lax.Precision.HIGHEST,
        preferred_element_type=jnp.float32,
    )
    return combined.astype(jnp.bfloat16)


def solution(mesh):
    in_specs = (
        P(("dp", "expert"), "tensor"),
        P(("dp", "expert"), None),
        P(("dp", "expert"), None),
        P("expert", None, ("dp", "tensor")),
        P("expert", None, ("dp", "tensor")),
        P("expert", "dp", "tensor"),
    )
    out_specs = P(("dp", "expert"), "tensor")
    return jax.shard_map(body, mesh=mesh, in_specs=in_specs, out_specs=out_specs, check_vma=False)
```

profile of v0, /device:TPU:0, one launch (start us, length us, event | category | flops | bytes accessed | tf_op | source)
XLA Modules:
  0.0 131.8 jit_solution(14651087666373031079)
XLA Ops:
  6.5 0.0 copy-start
  6.5 0.0 all-gather.3.cloned.1.call-start
  6.5 0.8 copy.13
  7.3 0.1 eq.71
  7.4 0.1 fusion.12
  7.5 0.1 reduce_window_sum.11
  7.6 0.2 select_reduce_fusion
  7.8 0.1 reduce_sum.12
  7.9 0.1 copy.14
  8.0 0.7 multiply_add_fusion
  8.7 0.0 copy-done
  8.7 0.2 convolution_convert_fusion
  8.9 8.6 %all_to_all.10 = bf16[4,16,1024]{2,1,0:T(8,128)(2,1)S(1)} all-to-all(bf16[4,16,1024]{2,1,0:T(8,128)(2,1)S(1)} %bitcast.31), channel_id=1, replica_groups=mesh['dp'=2,'expert'=4,'tensor'=4] {'expert'}, dimensions={0} | all-to-all | bytes 262144 | tf_op jit(solution)/shard_map/all_to_all | solution.py:37
  17.5 16.2 %all_gather.9 = bf16[64,4096]{1,0:T(8,128)(2,1)} all-gather(bf16[64,1024]{1,0:T(8,128)(2,1)S(1)} %bitcast.30), channel_id=1, replica_groups=mesh['dp'=2,'expert'=4,'tensor'=4] {'tensor'}, dimensions={1}, use_global_device_ids=true | all-gather | bytes 655360 | tf_op jit(solution)/shard_map/all_gather | solution.py:43
  33.8 0.0 all-gather.3.cloned.1.call-update
  33.8 0.0 all-gather.5.cloned.1.call-start
  33.8 22.4 %all-gather.3.cloned.1.call-done = bf16[128,4096]{1,0:T(8,128)(2,1)} async-done(((bf16[64,4096]{1,0:T(8,128)(2,1)}), bf16[128,4096]{1,0:T(8,128)(2,1)}) %all-gather.3.cloned.1.call-update) | async-done | bytes 1048592 | tf_op jit(solution)/shard_map/all_gather | solution.py:44
  56.2 0.0 copy-start.1
  56.2 5.0 %fusion.4 = f32[128,1024]{1,0:T(8,128)S(1)} fusion(bf16[128,4096]{1,0:T(8,128)(2,1)} %all-gather.3.cloned.1.call-done, bf16[1,4096,1024]{2,1,0:T(8,128)(2,1)} %param.9), kind=kOutput, calls=%fused_computation.4 | convolution fusion | flops 1073741824 | bytes 9961472 | tf_op jit(solution)/shard_map/dot_general | solution.py:45
  61.2 0.0 copy-done.1
  61.2 5.5 %fusion.9 = bf16[128,1024]{1,0:T(8,128)(2,1)} fusion(bf16[128,4096]{1,0:T(8,128)(2,1)S(1)} %copy-done.1, bf16[1,4096,1024]{2,1,0:T(8,128)(2,1)} %param.10, f32[128,1024]{1,0:T(8,128)S(1)} %fusion.4), kind=kOutput, calls=%fused_computation.7 | convolution fusion | flops 1074528256 | bytes 10223616 | tf_op jit(solution)/shard_map/dot_general | solution.py:46
  66.7 0.0 all-gather.5.cloned.1.call-update
  66.8 0.0 copy-start.2
  66.8 0.0 reduce-scatter.2.cloned.1.call-start
  66.8 28.0 %all-gather.5.cloned.1.call-done = bf16[128,4096]{1,0:T(8,128)(2,1)} async-done(((bf16[128,1024]{1,0:T(8,128)(2,1)}), bf16[128,4096]{1,0:T(8,128)(2,1)}) %all-gather.5.cloned.1.call-update) | async-done | bytes 1048592 | tf_op jit(solution)/shard_map/all_gather | solution.py:48
  94.8 5.8 %fusion = f32[128,1024]{1,0:T(8,128)} fusion(bf16[128,4096]{1,0:T(8,128)(2,1)} %all-gather.5.cloned.1.call-done, bf16[1,4096,1024]{2,1,0:T(8,128)(2,1)} %param.11), kind=kOutput, calls=%fused_computation | convolution fusion | flops 1073741824 | bytes 9961472 | tf_op jit(solution)/shard_map/dot_general | solution.py:50
  100.6 0.0 reduce-scatter.2.cloned.1.call-update
  100.7 14.2 %reduce-scatter.2.cloned.1.call-done = f32[64,1024]{1,0:T(8,128)} async-done(((f32[128,1024]{1,0:T(8,128)}), f32[64,1024]{1,0:T(8,128)}) %reduce-scatter.2.cloned.1.call-update) | async-done | bytes 262160 | tf_op jit(solution)/shard_map/reduce_scatter | solution.py:49
  114.9 1.6 %convert_element_type.31 = bf16[64,1024]{1,0:T(8,128)(2,1)} convert(f32[64,1024]{1,0:T(8,128)} %reduce-scatter.2.cloned.1.call-done) | non-fusion elementwise | flops 65536 | bytes 393216 | tf_op jit(solution)/shard_map/convert_element_type | solution.py:55
  116.5 3.3 %all-to-all-start.1 = ((bf16[4,16,1024]{2,1,0:T(8,128)(2,1)}), bf16[4,16,1024]{2,1,0:T(8,128)(2,1)S(1)}, u32[]{:S(2)}, u32[]{:S(2)}) async-start(bf16[4,16,1024]{2,1,0:T(8,128)(2,1)} %bitcast.9), calls=%async_computation.2 | async-start | bytes 262144 | tf_op jit(solution)/shard_map/all_to_all | solution.py:56
  119.8 0.0 copy-done.2
  119.8 4.6 %all-to-all-done.1 = bf16[4,16,1024]{2,1,0:T(8,128)(2,1)S(1)} async-done(((bf16[4,16,1024]{2,1,0:T(8,128)(2,1)}), bf16[4,16,1024]{2,1,0:T(8,128)(2,1)S(1)}, u32[]{:S(2)}, u32[]{:S(2)}) %all-to-all-start.1) | async-done | bytes 131104 | tf_op jit(solution)/shard_map/all_to_all | solution.py:56
  124.4 0.9 convolution_convert_fusion.1
  (2 shorter events, 0.0 us)
Async XLA Ops:
  6.5 2.2 %copy-start = (bf16[32,1024]{1,0:T(8,128)(2,1)S(1)}, bf16[32,1024]{1,0:T(8,128)(2,1)}, u32[]{:S(2)}) copy-start(bf16[32,1024]{1,0:T(8,128)(2,1)} %param.6) | copy-start | bytes 196612
  6.5 49.7 %all-gather.3.cloned.1.call-start = ((), (), s32[]{:S(2)}) async-start(), calls=%async_computation.3 | async-start | bytes 1572864 | tf_op jit(solution)/shard_map/all_gather | solution.py:44
  33.8 61.1 %all-gather.5.cloned.1.call-start = ((), (), s32[]{:S(2)}) async-start(), calls=%async_computation.4 | async-start | bytes 1310720 | tf_op jit(solution)/shard_map/all_gather | solution.py:48
  56.2 5.0 %copy-start.1 = (bf16[128,4096]{1,0:T(8,128)(2,1)S(1)}, bf16[128,4096]{1,0:T(8,128)(2,1)}, u32[]{:S(2)}) copy-start(bf16[128,4096]{1,0:T(8,128)(2,1)} %all-gather.3.cloned.1.call-done) | copy-start | bytes 3145732
  66.8 53.1 %copy-start.2 = (f32[32,2]{0,1:T(2,128)S(1)}, f32[32,2]{0,1:T(2,128)}, u32[]{:S(2)}) copy-start(f32[32,2]{0,1:T(2,128)} %param.8) | copy-start | bytes 772
  66.8 48.1 %reduce-scatter.2.cloned.1.call-start = ((), (), s32[]{:S(2)}) async-start(), calls=%async_computation.5 | async-start | bytes 786432 | tf_op jit(solution)/shard_map/reduce_scatter | solution.py:49
  116.5 7.9 %all-to-all-start.1 = ((bf16[4,16,1024]{2,1,0:T(8,128)(2,1)}), bf16[4,16,1024]{2,1,0:T(8,128)(2,1)S(1)}, u32[]{:S(2)}, u32[]{:S(2)}) async-start(bf16[4,16,1024]{2,1,0:T(8,128)(2,1)} %bitcast.9), calls=%async_computation.2 | async-start | bytes 262144 | tf_op jit(solution)/shard_map/all_to_all | solution.py:56
Sparse Core Ops, SparseCore 0:
  33.9 22.2 all-gather.2
  66.9 27.9 all-gather.4
  100.8 14.0 reduce-scatter.1
where the time goes:
time: 132 us
  waiting for transfers between devices  69.2 us (52%)
  blocking collectives  24.9 us (19%)
  matrix products  17.4 us (13%)
  between operations  13.2 us (10%)
  starting transfers between devices  3.41 us (3%)
  other arithmetic  2.66 us (2%)
    all_gather x1, waiting for transfers between devices, body(): unit_rows = lax.all_gather(activated, 'tensor', axis=1, tiled=True)  28 us
    all_gather x1, waiting for transfers between devices, body(): shards = lax.all_gather(features, 'dp', axis=0, tiled=True)  22.4 us
    all_gather x1, blocking collectives, body(): features = lax.all_gather(arrived, 'tensor', axis=1, tiled=True)  16.2 us
    reduce_scatter x1, waiting for transfers between devices, body(): lax.psum_scatter(jnp.dot(unit_rows, down_weights, preferred_element_type=...  14.2 us
    all_to_all x1, blocking collectives, body(): lax.all_to_all(packed, 'expert', split_axis=0, concat_axis=0, tiled=True)  8.64 us
    dot_general x1, matrix products, body(): jnp.dot(unit_rows, down_weights, preferred_element_type=jnp.float32)  5.79 us
    dot_general x1, matrix products, body(): up_part = jnp.dot(shards, up_weights, preferred_element_type=jnp.float32)  5.48 us
    dot_general x1, matrix products, body(): jnp.dot(shards, gate_weights, preferred_element_type=jnp.float32)  5.03 us
  transfers between devices with their start and end apart: 4, of which 4 were waited for; matrix products, arithmetic and copies ran while one was open for 0% of the time, Pallas kernels for 0%

commit v1 on v0

--- a/solution.py
+++ b/solution.py
@@ -1,9 +1,42 @@
+import functools
 import jax
 import jax.numpy as jnp
 from jax import lax
 from jax.sharding import PartitionSpec as P
 
 CAP = 16
+
+
+def connect_sites_here(values, which_dim):
+    low = jax.lax.axis_size("tensor")
+    current_arr, kept_arr, found_now = (low, jax.lax.axis_index("tensor"), values.shape[which_dim])
+    fields = []
+    for jj, s in enumerate(values.shape):
+        fields.append(s * current_arr if jj == which_dim else s)
+    local_out = lax.dynamic_update_slice_in_dim(
+        jnp.zeros(fields, values.dtype), values, kept_arr * found_now, axis=which_dim
+    )
+    mid_arr = state_now = values
+    for u in range(1, current_arr // 2 + 1):
+        kept_rows = []
+        for jj in range(current_arr):
+            kept_rows.append((jj, (jj + 1) % current_arr))
+        mid_arr = jax.lax.ppermute(mid_arr, "tensor", kept_rows)
+        local_out = lax.dynamic_update_slice_in_dim(
+            local_out, mid_arr, (kept_arr - u) % current_arr * found_now, axis=which_dim
+        )
+        if 2 * u < current_arr:
+            rows = []
+            for jj in range(current_arr):
+                rows.append((jj, (jj - 1) % current_arr))
+            state_now = jax.lax.ppermute(state_now, "tensor", rows)
+            local_out = lax.dynamic_update_slice_in_dim(
+                local_out, state_now, (kept_arr + u) % current_arr * found_now, axis=which_dim
+            )
+    return local_out
+
+
+check_ticks = functools.partial(connect_sites_here, which_dim=1)
 
 
 def slot_tables(chosen_experts, experts, capacity):
@@ -40,7 +73,7 @@
     gate_weights = gate_proj[0]
     up_weights = up_proj[0]
     down_weights = down_proj[0]
-    features = lax.all_gather(arrived, "tensor", axis=1, tiled=True)
+    features = check_ticks(arrived)
     shards = lax.all_gather(features, "dp", axis=0, tiled=True)
     gate_part = jnp.dot(shards, gate_weights, preferred_element_type=jnp.float32)
     up_part = jnp.dot(shards, up_weights, preferred_element_type=jnp.float32)

time: 132 us -> 129 us (0.977)
  blocking collectives: 24.9 us -> 8.64 us
  waiting for transfers between devices: 69.2 us -> 77.4 us
  starting transfers between devices: 3.41 us -> 7.23 us
    all_gather x1 -> x0, blocking collectives: 16.2 us -> none  [body(): features = lax.all_gather(arrived, 'tensor', axis=1, tiled=True)]
    ppermute x0 -> x3, waiting for transfers between devices: none -> 11 us  [the longest x2 10.2 us: connect_sites_here(): mid_arr = jax.lax.ppermute(mid_arr, 'tensor', kept_rows)]
    ppermute x0 -> x3, starting transfers between devices: none -> 3.83 us  [the longest x1 2.25 us: connect_sites_here(): state_now = jax.lax.ppermute(state_now, 'tensor', rows)]
    all_gather x1, waiting for transfers between devices: 22.4 us -> 19.6 us  [body(): shards = lax.all_gather(features, 'dp', axis=0, tiled=True)]
  transfers between devices with their start and end apart: 4 -> 7, of which waited for: 4 -> 7; matrix products, arithmetic and copies ran while one was open for 0% -> 0% of each run, Pallas kernels for 0% -> 0%
where the time goes in v1:
time: 129 us
  waiting for transfers between devices  77.4 us (60%)
  matrix products  17.4 us (13%)
  between operations  13.2 us (10%)
  blocking collectives  8.64 us (7%)
  starting transfers between devices  7.23 us (6%)
  other arithmetic  2.66 us (2%)
  local copies, waits for them, and re-layouts  2 us (2%)
    all_gather x1, waiting for transfers between devices, body(): unit_rows = lax.all_gather(activated, 'tensor', axis=1, tiled=True)  28 us
    all_gather x1, waiting for transfers between devices, body(): shards = lax.all_gather(features, 'dp', axis=0, tiled=True)  19.6 us
    reduce_scatter x1, waiting for transfers between devices, body(): lax.psum_scatter(jnp.dot(unit_rows, down_weights, preferred_element_type=...  14.2 us
    ppermute x2, waiting for transfers between devices, connect_sites_here(): mid_arr = jax.lax.ppermute(mid_arr, 'tensor', kept_rows)  10.2 us
    all_to_all x1, blocking collectives, body(): lax.all_to_all(packed, 'expert', split_axis=0, concat_axis=0, tiled=True)  8.64 us
    dot_general x1, matrix products, body(): jnp.dot(unit_rows, down_weights, preferred_element_type=jnp.float32)  5.79 us
    dot_general x1, matrix products, body(): up_part = jnp.dot(shards, up_weights, preferred_element_type=jnp.float32)  5.49 us
    dot_general x1, matrix products, body(): jnp.dot(shards, gate_weights, preferred_element_type=jnp.float32)  5.03 us
  transfers between devices with their start and end apart: 7, of which 7 were waited for; matrix products, arithmetic and copies ran while one was open for 0% of the time, Pallas kernels for 0%

profile of v1, /device:TPU:0, one launch (start us, length us, event | category | flops | bytes accessed | tf_op | source)
XLA Modules:
  0.0 128.6 jit_solution(5760717315470923389)
XLA Ops:
  6.5 0.0 copy-start
  6.5 0.0 all-gather.3.cloned.1.call-start
  6.5 0.8 copy.13
  7.3 0.1 eq.75
  7.4 0.1 fusion.6
  7.5 0.1 reduce_window_sum.11
  7.6 0.2 select_reduce_fusion
  7.8 0.1 reduce_sum.12
  7.9 0.1 copy.14
  8.0 0.7 multiply_add_fusion
  8.7 0.0 copy-done
  8.7 0.2 convolution_convert_fusion
  8.9 8.6 %all_to_all.10 = bf16[4,16,1024]{2,1,0:T(8,128)(2,1)S(1)} all-to-all(bf16[4,16,1024]{2,1,0:T(8,128)(2,1)S(1)} %bitcast.31), channel_id=1, replica_groups=mesh['dp'=2,'expert'=4,'tensor'=4] {'expert'}, dimensions={0} | all-to-all | bytes 262144 | tf_op jit(solution)/shard_map/all_to_all | solution.py:70
  17.5 1.6 %collective-permute-start = (bf16[64,1024]{1,0:T(8,128)(2,1)S(1)}, bf16[64,1024]{1,0:T(8,128)(2,1)S(1)}, u32[]{:S(2)}, u32[]{:S(2)}) collective-permute-start(bf16[64,1024]{1,0:T(8,128)(2,1)S(1)} %bitcast.28), channel_id=1, source_target_pairs={{0,1},{1,2},{2,3},{3,0},{4,5},{5,6},{6,7},{7,4},{8,9},{9,10},{10,1... | collective-permute-start | bytes 393224 | tf_op jit(solution)/shard_map/ppermute | solution.py:24
  19.1 2.2 %collective-permute-start.1 = (bf16[64,1024]{1,0:T(8,128)(2,1)S(1)}, bf16[64,1024]{1,0:T(8,128)(2,1)S(1)}, u32[]{:S(2)}, u32[]{:S(2)}) collective-permute-start(bf16[64,1024]{1,0:T(8,128)(2,1)S(1)} %bitcast.29), channel_id=1, source_target_pairs={{0,3},{1,0},{2,1},{3,2},{4,7},{5,4},{6,5},{7,6},{8,11},{9,8},{10,9... | collective-permute-start | bytes 393224 | tf_op jit(solution)/shard_map/ppermute | solution.py:32
  21.4 4.3 %collective-permute-done = bf16[64,1024]{1,0:T(8,128)(2,1)S(1)} collective-permute-done((bf16[64,1024]{1,0:T(8,128)(2,1)S(1)}, bf16[64,1024]{1,0:T(8,128)(2,1)S(1)}, u32[]{:S(2)}, u32[]{:S(2)}) %collective-permute-start) | collective-permute-done | bytes 131104 | tf_op jit(solution)/shard_map/ppermute | solution.py:24
  25.7 0.0 collective-permute-start.2
  25.7 0.8 collective-permute-done.1
  26.5 5.9 %collective-permute-done.2 = bf16[64,1024]{1,0:T(8,128)(2,1)S(1)} collective-permute-done((bf16[64,1024]{1,0:T(8,128)(2,1)S(1)}, bf16[64,1024]{1,0:T(8,128)(2,1)S(1)}, u32[]{:S(2)}, u32[]{:S(2)}) %collective-permute-start.2) | collective-permute-done | bytes 131104 | tf_op jit(solution)/shard_map/ppermute | solution.py:24
  32.4 0.0 copy-start.2
  32.5 0.8 copy-done.2
  33.3 0.0 all-gather.3.cloned.1.call-update
  33.3 0.0 all-gather.5.cloned.1.call-start
  33.3 19.6 %all-gather.3.cloned.1.call-done = bf16[128,4096]{1,0:T(8,128)(2,1)} async-done(((bf16[64,4096]{1,0:T(8,128)(2,1)}), bf16[128,4096]{1,0:T(8,128)(2,1)}) %all-gather.3.cloned.1.call-update) | async-done | bytes 1048592 | tf_op jit(solution)/shard_map/all_gather | solution.py:77
  52.9 0.0 copy-start.1
  52.9 5.0 %fusion.4 = f32[128,1024]{1,0:T(8,128)S(1)} fusion(bf16[128,4096]{1,0:T(8,128)(2,1)} %all-gather.3.cloned.1.call-done, bf16[1,4096,1024]{2,1,0:T(8,128)(2,1)} %param.9), kind=kOutput, calls=%fused_computation.4 | convolution fusion | flops 1073741824 | bytes 9961472 | tf_op jit(solution)/shard_map/dot_general | solution.py:78
  58.0 0.0 copy-done.1
  58.0 5.5 %multiply_convert_fusion = bf16[128,1024]{1,0:T(8,128)(2,1)} fusion(f32[128,1024]{1,0:T(8,128)S(1)} %fusion.4, bf16[128,4096]{1,0:T(8,128)(2,1)S(1)} %copy-done.1, bf16[1,4096,1024]{2,1,0:T(8,128)(2,1)} %param.10), kind=kOutput, calls=%fused_computation.8 | convolution fusion | flops 1074528256 | bytes 10223616 | tf_op jit(solution)/shard_map/dot_general | solution.py:79
  63.5 0.0 all-gather.5.cloned.1.call-update
  63.5 0.0 copy-start.3
  63.5 0.0 reduce-scatter.2.cloned.1.call-start
  63.6 28.0 %all-gather.5.cloned.1.call-done = bf16[128,4096]{1,0:T(8,128)(2,1)} async-done(((bf16[128,1024]{1,0:T(8,128)(2,1)}), bf16[128,4096]{1,0:T(8,128)(2,1)}) %all-gather.5.cloned.1.call-update) | async-done | bytes 1048592 | tf_op jit(solution)/shard_map/all_gather | solution.py:81
  91.6 5.8 %fusion = f32[128,1024]{1,0:T(8,128)} fusion(bf16[128,4096]{1,0:T(8,128)(2,1)} %all-gather.5.cloned.1.call-done, bf16[1,4096,1024]{2,1,0:T(8,128)(2,1)} %param.11), kind=kOutput, calls=%fused_computation | convolution fusion | flops 1073741824 | bytes 9961472 | tf_op jit(solution)/shard_map/dot_general | solution.py:83
  97.4 0.0 reduce-scatter.2.cloned.1.call-update
  97.4 14.2 %reduce-scatter.2.cloned.1.call-done = f32[64,1024]{1,0:T(8,128)} async-done(((f32[128,1024]{1,0:T(8,128)}), f32[64,1024]{1,0:T(8,128)}) %reduce-scatter.2.cloned.1.call-update) | async-done | bytes 262160 | tf_op jit(solution)/shard_map/reduce_scatter | solution.py:82
  111.6 1.6 %convert_element_type.31 = bf16[64,1024]{1,0:T(8,128)(2,1)} convert(f32[64,1024]{1,0:T(8,128)} %reduce-scatter.2.cloned.1.call-done) | non-fusion elementwise | flops 65536 | bytes 393216 | tf_op jit(solution)/shard_map/convert_element_type | solution.py:88
  113.2 3.3 %all-to-all-start.1 = ((bf16[4,16,1024]{2,1,0:T(8,128)(2,1)}), bf16[4,16,1024]{2,1,0:T(8,128)(2,1)S(1)}, u32[]{:S(2)}, u32[]{:S(2)}) async-start(bf16[4,16,1024]{2,1,0:T(8,128)(2,1)} %bitcast.9), calls=%async_computation.2 | async-start | bytes 262144 | tf_op jit(solution)/shard_map/all_to_all | solution.py:89
  116.5 0.0 copy-done.3
  116.6 4.6 %all-to-all-done.1 = bf16[4,16,1024]{2,1,0:T(8,128)(2,1)S(1)} async-done(((bf16[4,16,1024]{2,1,0:T(8,128)(2,1)}), bf16[4,16,1024]{2,1,0:T(8,128)(2,1)S(1)}, u32[]{:S(2)}, u32[]{:S(2)}) %all-to-all-start.1) | async-done | bytes 131104 | tf_op jit(solution)/shard_map/all_to_all | solution.py:89
  121.1 0.9 convolution_convert_fusion.1
  (7 shorter events, 0.1 us)
Async XLA Ops:
  6.5 2.2 %copy-start = (bf16[32,1024]{1,0:T(8,128)(2,1)S(1)}, bf16[32,1024]{1,0:T(8,128)(2,1)}, u32[]{:S(2)}) copy-start(bf16[32,1024]{1,0:T(8,128)(2,1)} %param.6) | copy-start | bytes 196612
  6.5 46.4 %all-gather.3.cloned.1.call-start = ((), (), s32[]{:S(2)}) async-start(), calls=%async_computation.3 | async-start | bytes 1572864 | tf_op jit(solution)/shard_map/all_gather | solution.py:77
  17.5 8.2 %collective-permute-start = (bf16[64,1024]{1,0:T(8,128)(2,1)S(1)}, bf16[64,1024]{1,0:T(8,128)(2,1)S(1)}, u32[]{:S(2)}, u32[]{:S(2)}) collective-permute-start(bf16[64,1024]{1,0:T(8,128)(2,1)S(1)} %bitcast.28), channel_id=1, source_target_pairs={{0,1},{1,2},{2,3},{3,0},{4,5},{5,6},{6,7},{7,4},{8,9},{9,10},{10,1... | collective-permute-start | bytes 393224 | tf_op jit(solution)/shard_map/ppermute | solution.py:24
  19.1 7.4 %collective-permute-start.1 = (bf16[64,1024]{1,0:T(8,128)(2,1)S(1)}, bf16[64,1024]{1,0:T(8,128)(2,1)S(1)}, u32[]{:S(2)}, u32[]{:S(2)}) collective-permute-start(bf16[64,1024]{1,0:T(8,128)(2,1)S(1)} %bitcast.29), channel_id=1, source_target_pairs={{0,3},{1,0},{2,1},{3,2},{4,7},{5,4},{6,5},{7,6},{8,11},{9,8},{10,9... | collective-permute-start | bytes 393224 | tf_op jit(solution)/shard_map/ppermute | solution.py:32
  25.7 6.8 %collective-permute-start.2 = (bf16[64,1024]{1,0:T(8,128)(2,1)S(1)}, bf16[64,1024]{1,0:T(8,128)(2,1)S(1)}, u32[]{:S(2)}, u32[]{:S(2)}) collective-permute-start(bf16[64,1024]{1,0:T(8,128)(2,1)S(1)} %collective-permute-done), channel_id=1, source_target_pairs={{0,1},{1,2},{2,3},{3,0},{4,5},{5,6},{6,7},{7,4},{8,9},{9,10},{10,1... | collective-permute-start | bytes 393224 | tf_op jit(solution)/shard_map/ppermute | solution.py:24
  32.4 0.8 copy-start.2
  33.3 58.3 %all-gather.5.cloned.1.call-start = ((), (), s32[]{:S(2)}) async-start(), calls=%async_computation.4 | async-start | bytes 1310720 | tf_op jit(solution)/shard_map/all_gather | solution.py:81
  52.9 5.0 %copy-start.1 = (bf16[128,4096]{1,0:T(8,128)(2,1)S(1)}, bf16[128,4096]{1,0:T(8,128)(2,1)}, u32[]{:S(2)}) copy-start(bf16[128,4096]{1,0:T(8,128)(2,1)} %all-gather.3.cloned.1.call-done) | copy-start | bytes 3145732
  63.5 53.1 %copy-start.3 = (f32[32,2]{0,1:T(2,128)S(1)}, f32[32,2]{0,1:T(2,128)}, u32[]{:S(2)}) copy-start(f32[32,2]{0,1:T(2,128)} %param.8) | copy-start | bytes 772
  63.5 48.1 %reduce-scatter.2.cloned.1.call-start = ((), (), s32[]{:S(2)}) async-start(), calls=%async_computation.5 | async-start | bytes 786432 | tf_op jit(solution)/shard_map/reduce_scatter | solution.py:82
  113.2 7.9 %all-to-all-start.1 = ((bf16[4,16,1024]{2,1,0:T(8,128)(2,1)}), bf16[4,16,1024]{2,1,0:T(8,128)(2,1)S(1)}, u32[]{:S(2)}, u32[]{:S(2)}) async-start(bf16[4,16,1024]{2,1,0:T(8,128)(2,1)} %bitcast.9), calls=%async_computation.2 | async-start | bytes 262144 | tf_op jit(solution)/shard_map/all_to_all | solution.py:89
Sparse Core Ops, SparseCore 0:
  33.4 19.4 all-gather.2
  63.6 27.9 all-gather.4
  97.5 14.0 reduce-scatter.1
